TPU v7x, 512 devices: a whole 4x8x8 slice. The times are simulated.
512 devices in a mesh: dp: 8 (over y), pipe: 4 (over z_lo), tensor: 16 (over z_hi, x, core).
Axes of the slice: x: 4, y: 8, z: 8 (z_hi: 2, z_lo: 4; z = z_hi * 4 + z_lo), core: 2. Of those that a mesh axis runs over, the one named last changes fastest.
Arguments:
- activations: bfloat16 [4, 1536, 4096], P('pipe', 'tensor', 'dp'), may hold values from -6 to 6
- upstream: bfloat16 [4, 1536, 4096], P('pipe', 'tensor', 'dp'), may hold values from -4 to 4
- gate_value: bfloat16 [4, 1536, 14336], P('pipe', 'dp', 'tensor'), may hold values from -6 to 6
- up_value: bfloat16 [4, 1536, 14336], P('pipe', 'dp', 'tensor'), may hold values from -6 to 6
- hidden_grad: bfloat16 [4, 1536, 14336], P('pipe', 'dp', 'tensor'), may hold values from -4 to 4
- gate_weight: bfloat16 [4, 4096, 14336], P('pipe', 'dp', 'tensor'), may hold values from -0.09375 to 0.09375
- up_weight: bfloat16 [4, 4096, 14336], P('pipe', 'dp', 'tensor'), may hold values from -0.09375 to 0.09375
- gate_mask: int32 [4, 32, 112], P('pipe', 'dp', 'tensor'), may hold values 0 or 1
- up_mask: int32 [4, 32, 112], P('pipe', 'dp', 'tensor'), may hold values 0 or 1
Outputs:
- gate_gradient: bfloat16 [4, 4096, 14336], P('pipe', 'dp', 'tensor')
- up_gradient: bfloat16 [4, 4096, 14336], P('pipe', 'dp', 'tensor')
- handed_back: bfloat16 [4, 1536, 4096], P('pipe', 'tensor', 'dp')
Inputs may be any that keep to these rules, and one draw needn't show every extreme that they name: gate_mask[s, i, j] keeps (1) or prunes (0) block (i, j) of gate_weight[s]. up_mask[s, i, j] keeps (1) or prunes (0) block (i, j) of up_weight[s].
All inputs are finite; a program needn't handle non-finite values.
Results may differ from a plain program's by a relative error of at most 0.0049.
Values may be sent and summed in bfloat16 or wider, within the bound.
A program may use at most 64 MiB of HBM per device.

v0:
```python
import jax
import jax.numpy as jnp
from jax import lax
from jax.sharding import PartitionSpec as P


def shifted(array, axis, by):
    devices = lax.axis_size(axis)
    pairs = [(i, i + by) for i in range(devices) if 0 <= i + by < devices]
    return lax.ppermute(array, axis, pairs)


def apply_blocks(matrix, keep_mask):
    rows_blocks, cols_blocks = keep_mask.shape
    shaped = matrix.reshape(
        rows_blocks, matrix.shape[0] // rows_blocks, cols_blocks, matrix.shape[1] // cols_blocks
    )
    return (shaped * keep_mask.astype(matrix.dtype)[:, None, :, None]).reshape(matrix.shape)


def per_device(
    activations,
    upstream,
    gate_value,
    up_value,
    hidden_grad,
    gate_weight,
    up_weight,
    gate_mask,
    up_mask,
):
    gathered = lax.all_gather(activations, "tensor", axis=1, tiled=True)[0]
    gate_float = gate_value[0].astype(jnp.float32)
    up_float = up_value[0].astype(jnp.float32)
    hidden_float = hidden_grad[0].astype(jnp.float32)
    gate_sigmoid = jax.nn.sigmoid(gate_float)
    up_delta = (hidden_float * gate_float * gate_sigmoid).astype(jnp.bfloat16)
    gate_delta = (
        hidden_float * up_float * gate_sigmoid * (1.0 + gate_float * (1.0 - gate_sigmoid))
    ).astype(jnp.bfloat16)
    gate_kept = apply_blocks(gate_weight[0], gate_mask[0])
    up_kept = apply_blocks(up_weight[0], up_mask[0])
    over_tokens = (((0,), (0,)), ((), ()))
    over_hidden = (((1,), (1,)), ((), ()))
    gate_piece = lax.all_gather(gate_delta, "dp", axis=0, tiled=True)
    up_piece = lax.all_gather(up_delta, "dp", axis=0, tiled=True)
    gate_acc = lax.dot_general(
        gathered, gate_piece, over_tokens, preferred_element_type=jnp.float32
    )
    up_acc = lax.dot_general(gathered, up_piece, over_tokens, preferred_element_type=jnp.float32)
    partial_rows = lax.dot_general(
        gate_piece, gate_kept, over_hidden, preferred_element_type=jnp.float32
    )
    partial_rows = partial_rows + lax.dot_general(
        up_piece, up_kept, over_hidden, preferred_element_type=jnp.float32
    )
    branch = partial_rows
    gate_acc, up_acc, branch = (gate_acc, up_acc, branch)
    own_rows = lax.psum_scatter(branch, "tensor", scatter_dimension=0, tiled=True)
    gate_gradient = apply_blocks(gate_acc, gate_mask[0]).astype(jnp.bfloat16)[None]
    up_gradient = apply_blocks(up_acc, up_mask[0]).astype(jnp.bfloat16)[None]
    section_grad = (upstream[0].astype(jnp.float32) + own_rows).astype(jnp.bfloat16)
    handed = shifted(section_grad, "pipe", -1)
    return (gate_gradient, up_gradient, handed[None])


def solution(mesh):
    return jax.shard_map(
        per_device,
        mesh=mesh,
        in_specs=(
            P("pipe", "tensor", "dp"),
            P("pipe", "tensor", "dp"),
            P("pipe", "dp", "tensor"),
            P("pipe", "dp", "tensor"),
            P("pipe", "dp", "tensor"),
            P("pipe", "dp", "tensor"),
            P("pipe", "dp", "tensor"),
            P("pipe", "dp", "tensor"),
            P("pipe", "dp", "tensor"),
        ),
        out_specs=(P("pipe", "dp", "tensor"), P("pipe", "dp", "tensor"), P("pipe", "tensor", "dp")),
        check_vma=False,
    )
```

profile of v0, /device:TPU:64, one launch (start us, length us, event | category | flops | bytes accessed | tf_op | source)
XLA Modules:
  0.0 296.9 jit_solution(10414191053938637605)
XLA Ops:
  7.2 0.0 copy-start
  7.2 0.0 copy-start.3
  7.2 0.0 copy-start.1
  7.2 0.0 all-gather.4.cloned.1.call-start
  7.2 2.5 fusion.29
  9.8 0.0 all-gather.4.cloned.1.call-update
  9.8 0.0 all-gather.8.cloned.1.call-start
  9.8 0.7 all-gather.8.cloned.1.call-update
  10.5 0.0 all-gather.6.cloned.1.call-start
  10.6 0.7 all-gather.6.cloned.1.call-update
  11.3 0.0 reduce-scatter.2.cloned.1.call-start
  11.3 0.8 convert_bitcast_fusion.3
  12.1 0.1 copy.19
  12.2 0.0 copy-done
  12.2 0.5 copy.18
  12.7 0.0 copy-done.3
  12.7 0.1 copy.21
  12.8 0.0 copy-done.1
  12.9 0.5 copy.20
  13.4 46.9 %all-gather.4.cloned.1.call-done = bf16[1536,896]{1,0:T(8,128)(2,1)} async-done(((bf16[192,896]{1,0:T(8,128)(2,1)}), bf16[1536,896]{1,0:T(8,128)(2,1)}) %all-gather.4.cloned.1.call-update) | async-done | bytes 2752528 | tf_op jit(solution)/shard_map/all_gather | solution.py:45
  60.3 0.3 mul.74
  60.6 5.3 %fusion.17 = f32[1536,512]{1,0:T(8,128)} fusion(bf16[1536,896]{1,0:T(8,128)(2,1)} %all-gather.4.cloned.1.call-done, bf16[112,8,4,128]{3,2,1,0:T(4,128)(2,1)S(1)} %bitcast.99, bf16[1,512,896]{1,2,0:T(8,128)(2,1)S(1)} %copy.18), kind=kOutput, calls=%fused_computation.17 | convolution fusion | flops 1409744896 | bytes 7733248 | tf_op jit(solution)/shard_map/dot_general | solution.py:51
  65.8 41.5 %all-gather.8.cloned.1.call-done = bf16[1536,896]{1,0:T(8,128)(2,1)} async-done(((bf16[192,896]{1,0:T(8,128)(2,1)}), bf16[1536,896]{1,0:T(8,128)(2,1)}) %all-gather.8.cloned.1.call-update) | async-done | bytes 2752528 | tf_op jit(solution)/shard_map/all_gather | solution.py:46
  107.3 0.3 mul.77
  107.6 6.2 %convolution_add_fusion = f32[1536,512]{1,0:T(8,128)} fusion(f32[1536,512]{1,0:T(8,128)} %fusion.17, bf16[1536,896]{1,0:T(8,128)(2,1)} %all-gather.8.cloned.1.call-done, bf16[112,8,4,128]{3,2,1,0:T(4,128)(2,1)S(1)} %bitcast.98, bf16[1,512,896]{1,2,0:T(8,128)(2,1)S(1)} %copy.20), kind=kOutput, calls=%fused_computation | convolution fusion | flops 1410531328 | bytes 10878976 | tf_op jit(solution)/shard_map/dot_general | solution.py:54
  113.8 0.0 reduce-scatter.2.cloned.1.call-update
  113.9 0.1 copy.16
  114.0 0.1 copy.17
  114.1 58.1 %all-gather.6.cloned.1.call-done = bf16[1,1536,512]{2,1,0:T(8,128)(2,1)} async-done(((bf16[1,96,512]{2,1,0:T(8,128)(2,1)}), bf16[1,1536,512]{2,1,0:T(8,128)(2,1)}) %all-gather.6.cloned.1.call-update) | async-done | bytes 1572880 | tf_op jit(solution)/shard_map/all_gather | solution.py:32
  172.2 0.3 mul.66
  172.5 0.0 copy-start.2
  172.5 3.9 %fusion.10 = bf16[1,512,896]{1,2,0:T(8,128)(2,1)S(1)} fusion(f32[112,8,4,128]{3,2,1,0:T(4,128)S(1)} %bitcast.97, bf16[1536,896]{1,0:T(8,128)(2,1)} %all-gather.4.cloned.1.call-done, bf16[1,1536,512]{2,1,0:T(8,128)(2,1)} %all-gather.6.cloned.1.call-done), kind=kOutput, calls=%fused_computation.9 | convolution fusion | flops 1410203648 | bytes 7077888 | tf_op jit(solution)/shard_map/dot_general | solution.py:47
  176.4 100.5 %reduce-scatter.2.cloned.1.call-done = f32[96,512]{1,0:T(8,128)} async-done(((f32[1536,512]{1,0:T(8,128)}), f32[96,512]{1,0:T(8,128)}) %reduce-scatter.2.cloned.1.call-update) | async-done | bytes 196624 | tf_op jit(solution)/shard_map/reduce_scatter | solution.py:59
  276.9 0.0 copy-done.2
  276.9 0.9 fusion.30
  277.9 5.2 %collective-permute-start = (bf16[96,512]{1,0:T(8,128)(2,1)S(1)}, bf16[96,512]{1,0:T(8,128)(2,1)S(1)}, u32[]{:S(2)}, u32[]{:S(2)}) collective-permute-start(bf16[96,512]{1,0:T(8,128)(2,1)S(1)} %fusion.30), channel_id=1, source_target_pairs={{16,0},{32,16},{48,32},{17,1},{33,17},{49,33},{18,2},{34,18},{50,3... | collective-permute-start | bytes 294920 | tf_op jit(solution)/shard_map/ppermute | solution.py:10
  283.1 0.3 mul.71
  283.4 3.8 %fusion.13 = bf16[1,512,896]{1,2,0:T(8,128)(2,1)S(1)} fusion(f32[112,8,4,128]{3,2,1,0:T(4,128)S(1)} %bitcast.96, bf16[1536,896]{1,0:T(8,128)(2,1)} %all-gather.8.cloned.1.call-done, bf16[1,1536,512]{2,1,0:T(8,128)(2,1)} %all-gather.6.cloned.1.call-done), kind=kOutput, calls=%fused_computation.10 | convolution fusion | flops 1410203648 | bytes 7077888 | tf_op jit(solution)/shard_map/dot_general | solution.py:50
  287.2 1.3 copy.22
  288.5 1.3 copy.23
  289.8 0.0 collective-permute-done
  289.8 0.6 copy.43
  (1 shorter events, 0.0 us)
Async XLA Ops:
  7.2 5.0 %copy-start = (bf16[1,512,896]{2,1,0:T(8,128)(2,1)S(1)}, bf16[1,512,896]{2,1,0:T(8,128)(2,1)}, u32[]{:S(2)}) copy-start(bf16[1,512,896]{2,1,0:T(8,128)(2,1)} %param.14) | copy-start | bytes 2752516
  7.2 5.5 %copy-start.3 = (s32[1,4,7]{2,1,0:T(4,128)S(1)}, s32[1,4,7]{2,1,0:T(4,128)}, u32[]{:S(2)}) copy-start(s32[1,4,7]{2,1,0:T(4,128)} %param.17) | copy-start | bytes 340
  7.2 5.7 %copy-start.1 = (bf16[1,512,896]{2,1,0:T(8,128)(2,1)S(1)}, bf16[1,512,896]{2,1,0:T(8,128)(2,1)}, u32[]{:S(2)}) copy-start(bf16[1,512,896]{2,1,0:T(8,128)(2,1)} %param.15) | copy-start | bytes 2752516
  7.2 53.1 %all-gather.4.cloned.1.call-start = ((), (), s32[]{:S(2)}) async-start(), calls=%async_computation.1 | async-start | bytes 3096576 | tf_op jit(solution)/shard_map/all_gather | solution.py:45
  9.8 97.5 %all-gather.8.cloned.1.call-start = ((), (), s32[]{:S(2)}) async-start(), calls=%async_computation.3 | async-start | bytes 3096576 | tf_op jit(solution)/shard_map/all_gather | solution.py:46
  10.5 161.7 %all-gather.6.cloned.1.call-start = ((), (), s32[]{:S(2)}) async-start(), calls=%async_computation.2 | async-start | bytes 1671168 | tf_op jit(solution)/shard_map/all_gather | solution.py:32
  11.3 265.7 %reduce-scatter.2.cloned.1.call-start = ((), (), s32[]{:S(2)}) async-start(), calls=%async_computation.4 | async-start | bytes 3342336 | tf_op jit(solution)/shard_map/reduce_scatter | solution.py:59
  172.5 104.4 %copy-start.2 = (bf16[1,96,512]{2,1,0:T(8,128)(2,1)S(1)}, bf16[1,96,512]{2,1,0:T(8,128)(2,1)}, u32[]{:S(2)}) copy-start(bf16[1,96,512]{2,1,0:T(8,128)(2,1)} %param.10) | copy-start | bytes 294916
  277.9 11.9 %collective-permute-start = (bf16[96,512]{1,0:T(8,128)(2,1)S(1)}, bf16[96,512]{1,0:T(8,128)(2,1)S(1)}, u32[]{:S(2)}, u32[]{:S(2)}) collective-permute-start(bf16[96,512]{1,0:T(8,128)(2,1)S(1)} %fusion.30), channel_id=1, source_target_pairs={{16,0},{32,16},{48,32},{17,1},{33,17},{49,33},{18,2},{34,18},{50,3... | collective-permute-start | bytes 294920 | tf_op jit(solution)/shard_map/ppermute | solution.py:10
Sparse Core Ops, SparseCore 0:
  10.7 49.5 all-gather.3
  62.9 44.3 all-gather.7
  110.6 61.5 all-gather.5
  176.9 99.9 reduce-scatter.1
where the time goes:
time: 297 us
  waiting for transfers between devices  248 us (84%)
  matrix products  19.2 us (6%)
  between operations  13.9 us (5%)
  local copies, waits for them, and re-layouts  5.86 us (2%)
  starting transfers between devices  5.31 us (2%)
  other arithmetic  4.23 us (1%)
    reduce_scatter x1, waiting for transfers between devices, per_device(): lax.psum_scatter(branch, 'tensor', scatter_dimension=0, tiled=True)  101 us
    all_gather x1, waiting for transfers between devices, per_device(): gathered = lax.all_gather(activations, 'tensor', axis=1, tiled=True)[0]  58.1 us
    all_gather x1, waiting for transfers between devices, per_device(): gate_piece = lax.all_gather(gate_delta, 'dp', axis=0, tiled=True)  46.9 us
    all_gather x1, waiting for transfers between devices, per_device(): up_piece = lax.all_gather(up_delta, 'dp', axis=0, tiled=True)  41.5 us
    dot_general x1, matrix products, per_device(): lax.dot_general(up_piece, up_kept, over_hidden, preferred_element_type=jn...  6.21 us
  transfers between devices with their start and end apart: 5, of which 4 were waited for; matrix products, arithmetic and copies ran while one was open for 8% of the time, Pallas kernels for 0%

commit v1 on v0

--- a/solution.py
+++ b/solution.py
@@ -42,8 +42,11 @@
     up_kept = apply_blocks(up_weight[0], up_mask[0])
     over_tokens = (((0,), (0,)), ((), ()))
     over_hidden = (((1,), (1,)), ((), ()))
-    gate_piece = lax.all_gather(gate_delta, "dp", axis=0, tiled=True)
-    up_piece = lax.all_gather(up_delta, "dp", axis=0, tiled=True)
+    gate_piece, up_piece = jnp.split(
+        lax.all_gather(jnp.concatenate([gate_delta, up_delta], axis=1), "dp", axis=0, tiled=True),
+        [gate_delta.shape[1]],
+        axis=1,
+    )
     gate_acc = lax.dot_general(
         gathered, gate_piece, over_tokens, preferred_element_type=jnp.float32
     )

time: 297 us -> 274 us (0.923)
  waiting for transfers between devices: 248 us -> 230 us
  matrix products: 19.2 us -> 15.2 us
    all_gather x2 -> x1, waiting for transfers between devices: 88.4 us -> 72.1 us  [per_device(): lax.all_gather(jnp.concatenate([gate_delta, up_delta], axis=1), 'dp', axi...]
  transfers between devices with their start and end apart: 5 -> 4, of which waited for: 4 -> 3; matrix products, arithmetic and copies ran while one was open for 8% -> 7% of each run, Pallas kernels for 0% -> 0%
where the time goes in v1:
time: 274 us
  waiting for transfers between devices  230 us (84%)
  matrix products  15.2 us (6%)
  between operations  13.9 us (5%)
  local copies, waits for them, and re-layouts  5.87 us (2%)
  starting transfers between devices  5.3 us (2%)
  other arithmetic  3.53 us (1%)
    reduce_scatter x1, waiting for transfers between devices, per_device(): lax.psum_scatter(branch, 'tensor', scatter_dimension=0, tiled=True)  101 us
    all_gather x1, waiting for transfers between devices, per_device(): lax.all_gather(jnp.concatenate([gate_delta, up_delta], axis=1), 'dp', axi...  72.1 us
    all_gather x1, waiting for transfers between devices, per_device(): gathered = lax.all_gather(activations, 'tensor', axis=1, tiled=True)[0]  56.8 us
  transfers between devices with their start and end apart: 4, of which 3 were waited for; matrix products, arithmetic and copies ran while one was open for 7% of the time, Pallas kernels for 0%

profile of v1, /device:TPU:64, one launch (start us, length us, event | category | flops | bytes accessed | tf_op | source)
XLA Modules:
  0.0 274.2 jit_solution(16650410235285140440)
XLA Ops:
  7.2 0.0 copy-start.3
  7.2 0.0 copy-start
  7.2 0.0 copy-start.4
  7.2 0.0 copy-start.1
  7.2 0.0 all-gather.3.cloned.1.call-start
  7.3 1.7 fusion.35
  8.9 0.9 pad_maximum_fusion
  9.8 0.0 all-gather.3.cloned.1.call-update
  9.9 0.0 all-gather.5.cloned.1.call-start
  9.9 0.7 all-gather.5.cloned.1.call-update
  10.6 0.0 reduce-scatter.2.cloned.1.call-start
  10.7 0.0 copy-done.3
  10.7 0.1 copy.19
  10.8 0.0 copy-done
  10.8 0.5 copy.18
  11.3 0.0 copy-done.4
  11.3 0.1 copy.21
  11.4 0.0 copy-done.1
  11.4 0.5 copy.20
  12.0 72.1 %all-gather.3.cloned.1.call-done = bf16[1536,1792]{1,0:T(8,128)(2,1)} async-done(((bf16[192,1792]{1,0:T(8,128)(2,1)}), bf16[1536,1792]{1,0:T(8,128)(2,1)}) %all-gather.3.cloned.1.call-update) | async-done | bytes 5505040 | tf_op jit(solution)/shard_map/all_gather | solution.py:46
  84.1 0.0 slice-start
  84.1 0.3 mul.74
  84.4 0.0 slice-start.1
  84.4 3.8 %fusion.3 = f32[1536,512]{1,0:T(8,128)S(1)} fusion(bf16[1536,1792]{1,0:T(8,128)(2,1)} %all-gather.3.cloned.1.call-done, bf16[112,8,4,128]{3,2,1,0:T(4,128)(2,1)S(1)} %bitcast.95, bf16[1,512,896]{1,2,0:T(8,128)(2,1)S(1)} %copy.18), kind=kOutput, calls=%fused_computation.4 | convolution fusion | flops 1409744896 | bytes 7733248 | tf_op jit(solution)/shard_map/dot_general | solution.py:54
  88.2 0.3 mul.77
  88.5 0.0 slice-done
  88.5 0.0 slice-done.1
  88.5 3.7 %convolution_add_fusion = f32[1536,512]{1,0:T(8,128)} fusion(f32[1536,512]{1,0:T(8,128)S(1)} %fusion.3, bf16[1536,1792]{1,0:T(8,128)(2,1)S(1)} %bitcast.98, bf16[112,8,4,128]{3,2,1,0:T(4,128)(2,1)S(1)} %bitcast.94, bf16[1,512,896]{1,2,0:T(8,128)(2,1)S(1)} %copy.20), kind=kOutput, calls=%fused_computation | convolution fusion | flops 1410531328 | bytes 10878976 | tf_op jit(solution)/shard_map/dot_general | solution.py:57
  92.2 0.0 reduce-scatter.2.cloned.1.call-update
  92.2 0.1 copy.17
  92.3 0.1 copy.16
  92.4 56.8 %all-gather.5.cloned.1.call-done = bf16[1,1536,512]{2,1,0:T(8,128)(2,1)} async-done(((bf16[1,96,512]{2,1,0:T(8,128)(2,1)}), bf16[1,1536,512]{2,1,0:T(8,128)(2,1)}) %all-gather.5.cloned.1.call-update) | async-done | bytes 1572880 | tf_op jit(solution)/shard_map/all_gather | solution.py:32
  149.3 0.3 mul.71
  149.6 0.0 copy-start.2
  149.6 3.9 %fusion.24 = bf16[1,512,896]{1,2,0:T(8,128)(2,1)S(1)} fusion(f32[112,8,4,128]{3,2,1,0:T(4,128)S(1)} %bitcast.93, bf16[1,1536,512]{2,1,0:T(8,128)(2,1)} %all-gather.5.cloned.1.call-done, bf16[1536,1792]{1,0:T(8,128)(2,1)} %all-gather.3.cloned.1.call-done), kind=kOutput, calls=%fused_computation.15 | convolution fusion | flops 1410203648 | bytes 7077888 | tf_op jit(solution)/shard_map/dot_general | solution.py:53
  153.5 100.7 %reduce-scatter.2.cloned.1.call-done = f32[96,512]{1,0:T(8,128)} async-done(((f32[1536,512]{1,0:T(8,128)}), f32[96,512]{1,0:T(8,128)}) %reduce-scatter.2.cloned.1.call-update) | async-done | bytes 196624 | tf_op jit(solution)/shard_map/reduce_scatter | solution.py:62
  254.2 0.0 copy-done.2
  254.2 0.9 fusion.42
  255.1 5.2 %collective-permute-start = (bf16[96,512]{1,0:T(8,128)(2,1)S(1)}, bf16[96,512]{1,0:T(8,128)(2,1)S(1)}, u32[]{:S(2)}, u32[]{:S(2)}) collective-permute-start(bf16[96,512]{1,0:T(8,128)(2,1)S(1)} %fusion.42), channel_id=1, source_target_pairs={{16,0},{32,16},{48,32},{17,1},{33,17},{49,33},{18,2},{34,18},{50,3... | collective-permute-start | bytes 294920 | tf_op jit(solution)/shard_map/ppermute | solution.py:10
  260.3 0.3 mul.68
  260.6 3.9 %fusion.19 = bf16[1,512,896]{1,2,0:T(8,128)(2,1)S(1)} fusion(f32[112,8,4,128]{3,2,1,0:T(4,128)S(1)} %bitcast.92, bf16[1,1536,512]{2,1,0:T(8,128)(2,1)} %all-gather.5.cloned.1.call-done, bf16[1536,1792]{1,0:T(8,128)(2,1)} %all-gather.3.cloned.1.call-done), kind=kOutput, calls=%fused_computation.14 | convolution fusion | flops 1410203648 | bytes 7077888 | tf_op jit(solution)/shard_map/dot_general | solution.py:50
  264.5 1.3 copy.23
  265.7 1.3 copy.22
  267.0 0.0 collective-permute-done
  267.0 0.6 copy.43
  (3 shorter events, 0.0 us)
Async XLA Ops:
  7.2 3.5 %copy-start.3 = (s32[1,4,7]{2,1,0:T(4,128)S(1)}, s32[1,4,7]{2,1,0:T(4,128)}, u32[]{:S(2)}) copy-start(s32[1,4,7]{2,1,0:T(4,128)} %param.16) | copy-start | bytes 340
  7.2 3.6 %copy-start = (bf16[1,512,896]{2,1,0:T(8,128)(2,1)S(1)}, bf16[1,512,896]{2,1,0:T(8,128)(2,1)}, u32[]{:S(2)}) copy-start(bf16[1,512,896]{2,1,0:T(8,128)(2,1)} %param.14) | copy-start | bytes 2752516
  7.2 4.1 %copy-start.4 = (s32[1,4,7]{2,1,0:T(4,128)S(1)}, s32[1,4,7]{2,1,0:T(4,128)}, u32[]{:S(2)}) copy-start(s32[1,4,7]{2,1,0:T(4,128)} %param.17) | copy-start | bytes 340
  7.2 4.3 %copy-start.1 = (bf16[1,512,896]{2,1,0:T(8,128)(2,1)S(1)}, bf16[1,512,896]{2,1,0:T(8,128)(2,1)}, u32[]{:S(2)}) copy-start(bf16[1,512,896]{2,1,0:T(8,128)(2,1)} %param.15) | copy-start | bytes 2752516
  7.2 76.9 %all-gather.3.cloned.1.call-start = ((), (), s32[]{:S(2)}) async-start(), calls=%async_computation.1 | async-start | bytes 6193152 | tf_op jit(solution)/shard_map/all_gather | solution.py:46
  9.9 139.4 %all-gather.5.cloned.1.call-start = ((), (), s32[]{:S(2)}) async-start(), calls=%async_computation.2 | async-start | bytes 1671168 | tf_op jit(solution)/shard_map/all_gather | solution.py:32
  10.6 243.5 %reduce-scatter.2.cloned.1.call-start = ((), (), s32[]{:S(2)}) async-start(), calls=%async_computation.3 | async-start | bytes 3342336 | tf_op jit(solution)/shard_map/reduce_scatter | solution.py:62
  84.1 4.4 %slice-start = ((s8[5505024]{0:T(1024)(128)(4,1)}), s8[4194304]{0:T(1024)(128)(4,1)S(1)}, s32[]{:S(2)}) async-start(s8[5505024]{0:T(1024)(128)(4,1)} %bitcast.97), calls=%async_computation.4 | async-start | bytes 8388608
  84.4 4.1 %slice-start.1 = ((s8[5505024]{0:T(1024)(128)(4,1)}), s8[1310720]{0:T(1024)(128)(4,1)S(1)}, s32[]{:S(2)}) async-start(s8[5505024]{0:T(1024)(128)(4,1)} %bitcast.97), calls=%async_computation.5 | async-start | bytes 2621440
  149.6 104.6 %copy-start.2 = (bf16[1,96,512]{2,1,0:T(8,128)(2,1)S(1)}, bf16[1,96,512]{2,1,0:T(8,128)(2,1)}, u32[]{:S(2)}) copy-start(bf16[1,96,512]{2,1,0:T(8,128)(2,1)} %param.10) | copy-start | bytes 294916
  255.1 11.9 %collective-permute-start = (bf16[96,512]{1,0:T(8,128)(2,1)S(1)}, bf16[96,512]{1,0:T(8,128)(2,1)S(1)}, u32[]{:S(2)}, u32[]{:S(2)}) collective-permute-start(bf16[96,512]{1,0:T(8,128)(2,1)S(1)} %fusion.42), channel_id=1, source_target_pairs={{16,0},{32,16},{48,32},{17,1},{33,17},{49,33},{18,2},{34,18},{50,3... | collective-permute-start | bytes 294920 | tf_op jit(solution)/shard_map/ppermute | solution.py:10
Sparse Core Ops, SparseCore 0:
  10.7 73.3 all-gather.2
  87.4 61.8 all-gather.4
  154.2 99.9 reduce-scatter.1
